TPU v7x, 32 devices: a whole 2x2x4 slice. The times are simulated.
32 devices in a mesh: row: 4 (over y, core), seq: 8 (over z, x).
Axes of the slice: x: 2, y: 2, z: 4, core: 2. Of those that a mesh axis runs over, the one named last changes fastest.
Arguments:
- tokens: bfloat16 [4, 2048, 1024], P('row', 'seq'), may hold values from -6 to 6
- cotangent: bfloat16 [4, 2048, 1024], P('row', 'seq'), may hold values from -6 to 6
- pair_lengths: int32 [4, 8], P('row'), may hold values from 1 to 513, 2048 in all within a row
- prefix_key: bfloat16 [64, 1024], replicated, may hold values from -6 to 6
- prefix_value: bfloat16 [64, 1024], replicated, may hold values from -6 to 6
- w_query: bfloat16 [1024, 1024], P('row'), may hold values from -0.1875 to 0.1875
- b_query: bfloat16 [1024], replicated, may hold values from -0.59765625 to 0.59765625
- w_key: bfloat16 [1024, 1024], P('row'), may hold values from -0.1875 to 0.1875
- w_value: bfloat16 [1024, 1024], P('row'), may hold values from -0.1875 to 0.1875
- b_value: bfloat16 [1024], replicated, may hold values from -0.29882812 to 0.29882812
- w_out: bfloat16 [1024, 1024], P('row'), may hold values from -1 to 1
- b_out: bfloat16 [1024], replicated, may hold values from -0.59765625 to 0.59765625
- gain_attn: bfloat16 [1024], replicated, may hold values from 0.5 to 1.5
- shift_attn: bfloat16 [1024], replicated, may hold values from -0.59765625 to 0.59765625
- w_up: bfloat16 [1024, 4096], P('row'), may hold values from -0.1875 to 0.1875
- b_up: bfloat16 [4096], replicated, may hold values from -0.59765625 to 0.59765625
- w_down: bfloat16 [4096, 1024], P('row'), may hold values from -0.09375 to 0.09375
- b_down: bfloat16 [1024], replicated, may hold values from -0.59765625 to 0.59765625
- gain_ffn: bfloat16 [1024], replicated, may hold values from 0.5 to 1.5
- shift_ffn: bfloat16 [1024], replicated, may hold values from -0.59765625 to 0.59765625
Outputs:
- out_tokens: bfloat16 [4, 2048, 1024], P('row', 'seq')
- grad_tokens: bfloat16 [4, 2048, 1024], P('row', 'seq')
- grad_prefix_key: float32 [64, 1024], replicated
- grad_prefix_value: float32 [64, 1024], replicated
Inputs may be any that keep to these rules, and one draw needn't show every extreme that they name: `pair_lengths`: each row's 8 pair lengths sum to 2048; in each row the longest pair has exactly 513 tokens.
All inputs are finite; a program needn't handle non-finite values.
Results may differ from a plain program's by a relative error of at most 0.02.
Values may be sent and summed in bfloat16 or wider, within the bound.
No kernel may reach another device: no remote copies, remote signals or barrier semaphores. Data moves between devices by JAX's collectives and lax.ppermute only.
A program may use at most 192 MiB of HBM per device.

v0:
```python
import jax
import jax.numpy as jnp
from jax import lax
from jax.sharding import PartitionSpec as P

HEADS = 16
HEAD_DIM = 64
REACH = 2
ln_eps = 1e-05
masked_fill = -1e30


def shifted(block, axis, distance):
    devices = range(lax.axis_size(axis))
    route = [(i - distance, i) for i in devices if i - distance in devices]
    return lax.ppermute(block, axis, route)


def shortened(value):
    return jax.tree.map(lambda a: a.astype(jnp.bfloat16) if a.dtype == jnp.float32 else a, value)


def layer_norm(field, gain_vec, shift_vec):
    average = jnp.mean(field, axis=-1, keepdims=True)
    centred = field - average
    variance = jnp.mean(centred * centred, axis=-1, keepdims=True)
    return centred * lax.rsqrt(variance + ln_eps) * gain_vec + shift_vec


def segment_ids(pair_ends, first_pos, tok_count, row_length):
    places = first_pos + jnp.arange(tok_count, dtype=jnp.int32)
    inside = (places >= 0) & (places < row_length)
    labels = jnp.sum((places[:, None] >= pair_ends[None, :]).astype(jnp.int32), axis=1)
    return jnp.where(inside, labels, -1)


def block_scores(queries, key_block, key_labels, query_labels, score_scale):
    scores = (
        jnp.einsum("qhd,khd->hqk", queries, key_block, preferred_element_type=jnp.float32)
        * score_scale
    )
    if key_labels is None:
        return scores
    allowed = query_labels[:, None] == key_labels[None, :]
    return jnp.where(allowed[None], scores, masked_fill)


def per_device(
    tokens,
    cotangent,
    pair_lengths,
    prefix_key,
    prefix_value,
    w_query,
    b_query,
    w_key,
    w_value,
    b_value,
    w_out,
    b_out,
    gain_attn,
    shift_attn,
    w_up,
    b_up,
    w_down,
    b_down,
    gain_ffn,
    shift_ffn,
):
    gathered = (
        lax.all_gather(w_query, "row", axis=0, tiled=True),
        lax.all_gather(w_key, "row", axis=0, tiled=True),
        lax.all_gather(w_value, "row", axis=0, tiled=True),
        lax.all_gather(w_out, "row", axis=0, tiled=True),
        lax.all_gather(w_up, "row", axis=0, tiled=True),
        lax.all_gather(w_down, "row", axis=0, tiled=True),
    )
    full_query, full_key, full_value, full_out, full_up, full_down = gathered
    inputs = tokens[0]
    tok_count = inputs.shape[0]
    width_model = inputs.shape[1]
    score_scale = HEAD_DIM ** (-0.5)
    position_index = lax.axis_index("seq")
    row_length = tok_count * lax.axis_size("seq")
    pair_ends = jnp.cumsum(pair_lengths[0])
    own_first = position_index * tok_count
    query_labels = segment_ids(pair_ends, own_first, tok_count, row_length)
    head_shape = (tok_count, HEADS, HEAD_DIM)
    query_proj = (
        jnp.dot(inputs, full_query, preferred_element_type=jnp.float32)
        + b_query.astype(jnp.float32)
    ).astype(jnp.bfloat16)
    key_proj = jnp.dot(inputs, full_key, preferred_element_type=jnp.float32).astype(jnp.bfloat16)
    value_proj = (
        jnp.dot(inputs, full_value, preferred_element_type=jnp.float32)
        + b_value.astype(jnp.float32)
    ).astype(jnp.bfloat16)
    queries = query_proj.reshape(head_shape)
    keys_own = key_proj.reshape(head_shape)
    values_own = value_proj.reshape(head_shape)
    prefix_count = prefix_key.shape[0]
    prefix_keys = prefix_key.reshape(prefix_count, HEADS, HEAD_DIM)
    prefix_values = prefix_value.reshape(prefix_count, HEADS, HEAD_DIM)

    def token_blocks(lowers, uppers):
        listing = [(keys_own, values_own, query_labels)]
        for distance in range(1, REACH + 1):
            lower_pair = lowers[distance - 1]
            upper_pair = uppers[distance - 1]
            listing.append(
                (
                    lower_pair[0],
                    lower_pair[1],
                    segment_ids(pair_ends, own_first - distance * tok_count, tok_count, row_length),
                )
            )
            listing.append(
                (
                    upper_pair[0],
                    upper_pair[1],
                    segment_ids(pair_ends, own_first + distance * tok_count, tok_count, row_length),
                )
            )
        return listing

    lower_list = []
    moving = (keys_own, values_own)
    for repeat in range(REACH):
        moving = shifted((moving[0], moving[1]), "seq", 1)
        lower_list.append(moving)
    upper_list = []
    moving = (keys_own, values_own)
    for repeat in range(REACH):
        moving = shifted((moving[0], moving[1]), "seq", -1)
        upper_list.append(moving)
    blocks = token_blocks(lower_list, upper_list)
    prefix_scores = block_scores(queries, prefix_keys, None, None, score_scale)
    running_max = jnp.max(prefix_scores, axis=-1)
    prefix_exp = jnp.exp(prefix_scores - running_max[..., None])
    running_sum = jnp.sum(prefix_exp, axis=-1)
    attended = jnp.einsum(
        "hqk,khd->qhd",
        prefix_exp.astype(jnp.bfloat16),
        prefix_values,
        preferred_element_type=jnp.float32,
    )
    for key_block, value_block, key_labels in blocks:
        scores = block_scores(queries, key_block, key_labels, query_labels, score_scale)
        new_max = jnp.maximum(running_max, jnp.max(scores, axis=-1))
        factor = jnp.exp(running_max - new_max)
        block_exp = jnp.exp(scores - new_max[..., None])
        running_sum = running_sum * factor + jnp.sum(block_exp, axis=-1)
        attended = attended * factor.T[..., None] + jnp.einsum(
            "hqk,khd->qhd",
            block_exp.astype(jnp.bfloat16),
            value_block,
            preferred_element_type=jnp.float32,
        )
        running_max = new_max
    log_total = running_max + jnp.log(running_sum)
    attended = attended / running_sum.T[..., None]
    attended_low = attended.reshape(tok_count, width_model).astype(jnp.bfloat16)

    def softmax_of(scores):
        return jnp.exp(scores - log_total[..., None])

    branch_attn = jnp.dot(
        attended_low, full_out, preferred_element_type=jnp.float32
    ) + b_out.astype(jnp.float32)
    hidden_in = inputs.astype(jnp.float32) + branch_attn
    gain_one = gain_attn.astype(jnp.float32)
    shift_one = shift_attn.astype(jnp.float32)
    normed = layer_norm(hidden_in, gain_one, shift_one)
    pre_act = jnp.dot(
        normed.astype(jnp.bfloat16), full_up, preferred_element_type=jnp.float32
    ) + b_up.astype(jnp.float32)
    activated = jax.nn.gelu(pre_act, approximate=False).astype(jnp.bfloat16)
    summed = (
        normed
        + jnp.dot(activated, full_down, preferred_element_type=jnp.float32)
        + b_down.astype(jnp.float32)
    )
    gain_two = gain_ffn.astype(jnp.float32)
    shift_two = shift_ffn.astype(jnp.float32)
    result = layer_norm(summed, gain_two, shift_two)
    upstream = cotangent[0].astype(jnp.float32)
    unused_out, pull_norm = jax.vjp(lambda field: layer_norm(field, gain_two, shift_two), summed)
    grad_summed = pull_norm(upstream)[0]
    grad_act = jnp.dot(
        grad_summed.astype(jnp.bfloat16), full_down.T, preferred_element_type=jnp.float32
    )
    unused_gelu, pull_gelu = jax.vjp(lambda field: jax.nn.gelu(field, approximate=False), pre_act)
    grad_pre = pull_gelu(grad_act)[0].astype(jnp.bfloat16)
    grad_normed = grad_summed + jnp.dot(grad_pre, full_up.T, preferred_element_type=jnp.float32)
    unused_first, pull_first = jax.vjp(
        lambda field: layer_norm(field, gain_one, shift_one), hidden_in
    )
    grad_hidden = pull_first(grad_normed)[0]
    grad_attended = (
        jnp.dot(grad_hidden.astype(jnp.bfloat16), full_out.T, preferred_element_type=jnp.float32)
        .astype(jnp.bfloat16)
        .reshape(head_shape)
    )
    inner_sum = jnp.sum(grad_attended.astype(jnp.float32) * attended, axis=-1).T
    again_lower = []
    moving = (keys_own, values_own)
    for repeat in range(REACH):
        moving = shifted((moving[0], moving[1]), "seq", 1)
        again_lower.append(moving)
    again_upper = []
    moving = (keys_own, values_own)
    for repeat in range(REACH):
        moving = shifted((moving[0], moving[1]), "seq", -1)
        again_upper.append(moving)
    back_blocks = token_blocks(again_lower, again_upper)

    def grad_probs_of(value_block):
        return jnp.einsum(
            "qhd,khd->hqk", grad_attended, value_block, preferred_element_type=jnp.float32
        )

    def score_grads(probs, grad_probs):
        return (probs * (grad_probs - inner_sum[..., None])).astype(jnp.bfloat16)

    prefix_probs = softmax_of(prefix_scores)
    prefix_grad_scores = score_grads(prefix_probs, grad_probs_of(prefix_values))
    grad_queries = jnp.einsum(
        "hqk,khd->qhd", prefix_grad_scores, prefix_keys, preferred_element_type=jnp.float32
    )
    grad_pkey = (
        jnp.einsum("hqk,qhd->khd", prefix_grad_scores, queries, preferred_element_type=jnp.float32)
        * score_scale
    )
    grad_pvalue = jnp.einsum(
        "hqk,qhd->khd",
        prefix_probs.astype(jnp.bfloat16),
        grad_attended,
        preferred_element_type=jnp.float32,
    )
    block_grads = []
    for key_block, value_block, key_labels in back_blocks:
        probs = softmax_of(block_scores(queries, key_block, key_labels, query_labels, score_scale))
        grad_scores = score_grads(probs, grad_probs_of(value_block))
        grad_queries = grad_queries + jnp.einsum(
            "hqk,khd->qhd", grad_scores, key_block, preferred_element_type=jnp.float32
        )
        key_grad = (
            jnp.einsum("hqk,qhd->khd", grad_scores, queries, preferred_element_type=jnp.float32)
            * score_scale
        )
        value_grad = jnp.einsum(
            "hqk,qhd->khd",
            probs.astype(jnp.bfloat16),
            grad_attended,
            preferred_element_type=jnp.float32,
        )
        block_grads.append((key_grad, value_grad))
    empty_grads = (jnp.zeros(head_shape, jnp.float32), jnp.zeros(head_shape, jnp.float32))
    carried = empty_grads
    for distance in range(REACH, 0, -1):
        carried = jax.tree.map(jnp.add, carried, block_grads[2 * distance - 1])
        carried = jax.tree.map(
            lambda part, own: part.astype(own.dtype),
            shifted(shortened(carried), "seq", -1),
            carried,
        )
    from_higher = carried
    carried = empty_grads
    for distance in range(REACH, 0, -1):
        carried = jax.tree.map(jnp.add, carried, block_grads[2 * distance])
        carried = jax.tree.map(
            lambda part, own: part.astype(own.dtype), shifted(shortened(carried), "seq", 1), carried
        )
    grad_keys = (
        (block_grads[0][0] + from_higher[0] + carried[0])
        .reshape(tok_count, width_model)
        .astype(jnp.bfloat16)
    )
    grad_values = (
        (block_grads[0][1] + from_higher[1] + carried[1])
        .reshape(tok_count, width_model)
        .astype(jnp.bfloat16)
    )
    grad_query_low = (
        (grad_queries * score_scale).reshape(tok_count, width_model).astype(jnp.bfloat16)
    )
    grad_inputs = grad_hidden + jnp.dot(
        grad_query_low, full_query.T, preferred_element_type=jnp.float32
    )
    grad_inputs = grad_inputs + jnp.dot(grad_keys, full_key.T, preferred_element_type=jnp.float32)
    grad_inputs = grad_inputs + jnp.dot(
        grad_values, full_value.T, preferred_element_type=jnp.float32
    )
    prefix_sums = lax.psum(
        (
            grad_pkey.reshape(prefix_count, width_model),
            grad_pvalue.reshape(prefix_count, width_model),
        ),
        ("row", "seq"),
    )
    return (
        result.astype(jnp.bfloat16)[None],
        grad_inputs.astype(jnp.bfloat16)[None],
        prefix_sums[0],
        prefix_sums[1],
    )


def solution(mesh):
    placed = (
        P("row", "seq", None),
        P("row", "seq", None),
        P("row", None),
        P(),
        P(),
        P("row", None),
        P(),
        P("row", None),
        P("row", None),
        P(),
        P("row", None),
        P(),
        P(),
        P(),
        P("row", None),
        P(),
        P("row", None),
        P(),
        P(),
        P(),
    )
    return jax.shard_map(
        per_device,
        mesh=mesh,
        in_specs=placed,
        out_specs=(P("row", "seq", None), P("row", "seq", None), P(), P()),
        check_vma=False,
    )
```

profile of v0, /device:TPU:0, one launch (start us, length us, event | category | flops | bytes accessed | tf_op | source)
XLA Modules:
  0.0 470.4 jit_solution(14875585755988890551)
XLA Ops:
  16.0 19.0 %all-gather.9.cloned.1.call-done = bf16[1024,1024]{1,0:T(8,128)(2,1)} async-done(((bf16[256,1024]{1,0:T(8,128)(2,1)}), bf16[1024,1024]{1,0:T(8,128)(2,1)}) %all-gather.9.cloned.1.call-update) | async-done | bytes 2097168 | tf_op jit(solution)/shard_map/all_gather | solution.py:72
  35.0 2.3 convolution_convert_fusion.1
  38.8 5.4 %collective-permute-start = (bf16[256,16,64]{0,2,1:T(8,128)(2,1)S(1)}, bf16[256,16,64]{0,2,1:T(8,128)(2,1)}, u32[]{:S(2)}, u32[]{:S(2)}) collective-permute-start(bf16[256,16,64]{0,2,1:T(8,128)(2,1)S(1)} %bitcast.310), channel_id=1, source_target_pairs={{0,1},{1,2},{2,3},{3,4},{4,5},{5,6},{6,7},{8,9},{9,10},{10,11},{11... | collective-permute-start | bytes 1572872 | tf_op jit(solution)/shard_map/ppermute | solution.py:16
  44.2 15.0 %all-gather.11.cloned.1.call-done = bf16[1024,1024]{1,0:T(8,128)(2,1)} async-done(((bf16[256,1024]{1,0:T(8,128)(2,1)}), bf16[1024,1024]{1,0:T(8,128)(2,1)}) %all-gather.11.cloned.1.call-update) | async-done | bytes 2097168 | tf_op jit(solution)/shard_map/all_gather | solution.py:73
  59.2 2.3 fusion.154
  63.8 5.3 %collective-permute-start.1 = (bf16[256,16,64]{0,2,1:T(8,128)(2,1)}, bf16[256,16,64]{0,2,1:T(8,128)(2,1)}, u32[]{:S(2)}, u32[]{:S(2)}) collective-permute-start(bf16[256,16,64]{0,2,1:T(8,128)(2,1)} %bitcast.8), channel_id=1, source_target_pairs={{0,1},{1,2},{2,3},{3,4},{4,5},{5,6},{6,7},{8,9},{9,10},{10,11},{11... | collective-permute-start | bytes 1572872 | tf_op jit(solution)/shard_map/ppermute | solution.py:16
  69.1 14.3 %all-gather.7.cloned.1.call-done = bf16[1024,1024]{1,0:T(8,128)(2,1)} async-done(((bf16[256,1024]{1,0:T(8,128)(2,1)}), bf16[1024,1024]{1,0:T(8,128)(2,1)}) %all-gather.7.cloned.1.call-update) | async-done | bytes 2097168 | tf_op jit(solution)/shard_map/all_gather | solution.py:71
  83.4 2.3 fusion.153
  88.7 4.6 collective-permute-start.4
  94.6 5.1 %collective-permute-start.5 = (bf16[256,16,64]{0,2,1:T(8,128)(2,1)}, bf16[256,16,64]{0,2,1:T(8,128)(2,1)S(1)}, u32[]{:S(2)}, u32[]{:S(2)}) collective-permute-start(bf16[256,16,64]{0,2,1:T(8,128)(2,1)} %collective-permute-done.1), channel_id=1, source_target_pairs={{0,1},{1,2},{2,3},{3,4},{4,5},{5,6},{6,7},{8,9},{9,10},{10,11},{11... | collective-permute-start | bytes 1572872 | tf_op jit(solution)/shard_map/ppermute | solution.py:16
  99.6 1.9 fusion.22
  102.4 23.4 %collective-permute-done.4 = bf16[256,16,64]{0,2,1:T(8,128)(2,1)S(1)} collective-permute-done((bf16[256,16,64]{0,2,1:T(8,128)(2,1)}, bf16[256,16,64]{0,2,1:T(8,128)(2,1)S(1)}, u32[]{:S(2)}, u32[]{:S(2)}) %collective-permute-start.4) | collective-permute-done | bytes 524320 | tf_op jit(solution)/shard_map/ppermute | solution.py:16
  132.4 2.2 fusion.89
  134.6 2.1 fusion.95
  138.2 2.2 fusion.145
  141.3 2.3 fusion.248
  143.6 2.7 fusion.249
  146.7 20.5 %all-gather.15.cloned.1.call-done = bf16[1024,4096]{1,0:T(8,128)(2,1)} async-done(((bf16[256,4096]{1,0:T(8,128)(2,1)}), bf16[1024,4096]{1,0:T(8,128)(2,1)}) %all-gather.15.cloned.1.call-update) | async-done | bytes 8388624 | tf_op jit(solution)/shard_map/all_gather | solution.py:75
  167.2 7.8 %convolution_add_fusion = f32[256,4096]{1,0:T(8,128)} fusion(bf16[1024,4096]{1,0:T(8,128)(2,1)} %all-gather.15.cloned.1.call-done, f32[4096]{0:T(1024)S(1)} %copy-done.48, f32[256,1024]{1,0:T(8,128)S(1)} %get-tuple-element.50, f32[1024]{0:T(1024)S(1)} %copy-done.59, f32[1024]{0:T(1024)S(1)} %copy-done.58, f32[256]{0:T(256)S(1)} %fusion.210, ...), kind=kOutput, calls=%fused_computation.1 | convolution fusion | flops 2149842944 | bytes 13658112 | tf_op jit(solution)/shard_map/dot_general | solution.py:174
  175.0 51.9 %all-gather.17.cloned.1.call-done = bf16[4096,1024]{1,0:T(8,128)(2,1)} async-done(((bf16[1024,1024]{1,0:T(8,128)(2,1)}), bf16[4096,1024]{1,0:T(8,128)(2,1)}) %all-gather.17.cloned.1.call-update) | async-done | bytes 8388624 | tf_op jit(solution)/shard_map/all_gather | solution.py:76
  226.9 14.3 %fusion.250 = (f32[256]{0:T(256)S(1)}, f32[256,1024]{1,0:T(8,128)S(1)}) fusion(f32[1024]{0:T(1024)} %convert_element_type.254, bf16[4096,1024]{1,0:T(8,128)(2,1)} %all-gather.17.cloned.1.call-done, f32[256,4096]{1,0:T(8,128)} %convolution_add_fusion, f32[1024]{0:T(1024)} %convert_element_type.250, f32[1024]{0:T(1024)} %convert_element_type.249, ...), kind=kOutput, calls=%fused_computation.306 | convolution fusion | flops 2217475840 | bytes 14695424 | tf_op jit(solution)/shard_map/dot_general | solution.py:180
  244.0 24.5 %multiply_reduce_fusion.1 = (f32[256]{0:T(256)}, f32[256,1024]{1,0:T(8,128)}) fusion(f32[256,1024]{1,0:T(8,128)S(1)} %get-tuple-element.50, f32[256]{0:T(256)} %copy-done.49, f32[1024]{0:T(1024)} %convert_element_type.249, bf16[1024,4096]{1,0:T(8,128)(2,1)} %all-gather.15.cloned.1.call-done, f32[256,4096]{1,0:T(8,128)} %convolution_add_fusion, ...), kind=kOutput, calls=%fused_computation.195 | convolution fusion | flops 4376231936 | bytes 24655872 | tf_op jit(solution)/shard_map/dot_general | solution.py:194
  271.8 2.3 convolution_convert_fusion
  275.5 4.4 fusion.168
  279.8 1.9 fusion.171
  282.2 2.0 fusion.104
  285.6 2.5 multiply_convert_fusion.4
  288.1 1.9 copy.145
  290.0 2.1 convolution_multiply_fusion.6
  292.1 1.9 copy.144
  294.1 3.8 multiply_convert_fusion
  305.1 6.0 %collective-permute-start.10 = (bf16[256,16,64]{0,2,1:T(8,128)(2,1)}, bf16[256,16,64]{0,2,1:T(8,128)(2,1)}, u32[]{:S(2)}, u32[]{:S(2)}) collective-permute-start(bf16[256,16,64]{0,2,1:T(8,128)(2,1)} %fusion.166), channel_id=1, source_target_pairs={{0,1},{1,2},{2,3},{3,4},{4,5},{5,6},{6,7},{8,9},{9,10},{10,11},{11... | collective-permute-start | bytes 1572872 | tf_op jit(solution)/shard_map/ppermute | solution.py:16
  311.0 5.0 %collective-permute-start.14 = (bf16[256,16,64]{0,2,1:T(8,128)(2,1)}, bf16[256,16,64]{0,2,1:T(8,128)(2,1)}, u32[]{:S(2)}, u32[]{:S(2)}) collective-permute-start(bf16[256,16,64]{0,2,1:T(8,128)(2,1)} %fusion.168), channel_id=1, source_target_pairs={{0,1},{1,2},{2,3},{3,4},{4,5},{5,6},{6,7},{8,9},{9,10},{10,11},{11... | collective-permute-start | bytes 1572872 | tf_op jit(solution)/shard_map/ppermute | solution.py:16
  317.9 2.2 convolution_bitcast_fusion
  320.2 3.8 multiply_convert_fusion.3
  324.0 2.6 multiply_convert_fusion.2
  327.2 1.8 fusion.119
  331.2 2.0 add_convert_fusion.11
  334.5 7.6 %collective-permute-done.10 = bf16[256,16,64]{0,2,1:T(8,128)(2,1)} collective-permute-done((bf16[256,16,64]{0,2,1:T(8,128)(2,1)}, bf16[256,16,64]{0,2,1:T(8,128)(2,1)}, u32[]{:S(2)}, u32[]{:S(2)}) %collective-permute-start.10) | collective-permute-done | bytes 524320 | tf_op jit(solution)/shard_map/ppermute | solution.py:16
  342.0 1.8 add_convert_fusion.10
  343.9 4.4 collective-permute-start.11
  348.3 2.2 add_convert_fusion.8
  351.9 13.2 %collective-permute-done.14 = bf16[256,16,64]{0,2,1:T(8,128)(2,1)} collective-permute-done((bf16[256,16,64]{0,2,1:T(8,128)(2,1)}, bf16[256,16,64]{0,2,1:T(8,128)(2,1)}, u32[]{:S(2)}, u32[]{:S(2)}) %collective-permute-start.14) | collective-permute-done | bytes 524320 | tf_op jit(solution)/shard_map/ppermute | solution.py:16
  365.1 2.2 add_convert_fusion.7
  367.3 4.6 collective-permute-start.15
  371.9 15.7 %collective-permute-done.11 = bf16[256,16,64]{0,2,1:T(8,128)(2,1)S(1)} collective-permute-done((bf16[256,16,64]{0,2,1:T(8,128)(2,1)S(1)}, bf16[256,16,64]{0,2,1:T(8,128)(2,1)S(1)}, u32[]{:S(2)}, u32[]{:S(2)}) %collective-permute-start.11) | collective-permute-done | bytes 524320 | tf_op jit(solution)/shard_map/ppermute | solution.py:16
  388.7 10.0 %collective-permute-done.15 = bf16[256,16,64]{0,2,1:T(8,128)(2,1)S(1)} collective-permute-done((bf16[256,16,64]{0,2,1:T(8,128)(2,1)S(1)}, bf16[256,16,64]{0,2,1:T(8,128)(2,1)S(1)}, u32[]{:S(2)}, u32[]{:S(2)}) %collective-permute-start.15) | collective-permute-done | bytes 524320 | tf_op jit(solution)/shard_map/ppermute | solution.py:16
  400.6 59.4 %all-reduce.3.cloned.1.call-done = (f32[64,1024]{1,0:T(8,128)}, f32[64,1024]{1,0:T(8,128)}) async-done(((f32[64,1024]{1,0:T(8,128)}, f32[64,1024]{1,0:T(8,128)}), (f32[64,1024]{1,0:T(8,128)}, f32[64,1024]{1,0:T(8,128)})) %all-reduce.3.cloned.1.call-update) | async-done | bytes 524304 | tf_op jit(solution)/shard_map/psum | solution.py:294
  (249 shorter events, 55.9 us)
Async XLA Ops:
  7.3 27.7 %copy-start.40 = (bf16[1,256,1024]{2,1,0:T(8,128)(2,1)S(1)}, bf16[1,256,1024]{2,1,0:T(8,128)(2,1)}, u32[]{:S(2)}) copy-start(bf16[1,256,1024]{2,1,0:T(8,128)(2,1)} %param.20) | copy-start | bytes 1572868
  7.3 27.7 %all-gather.9.cloned.1.call-start = ((), (), s32[]{:S(2)}) async-start(), calls=%async_computation.1 | async-start | bytes 2621440 | tf_op jit(solution)/shard_map/all_gather | solution.py:72
  8.0 51.2 %all-gather.11.cloned.1.call-start = ((), (), s32[]{:S(2)}) async-start(), calls=%async_computation.2 | async-start | bytes 2621440 | tf_op jit(solution)/shard_map/all_gather | solution.py:73
  8.8 74.6 %all-gather.7.cloned.1.call-start = ((), (), s32[]{:S(2)}) async-start(), calls=%async_computation | async-start | bytes 2621440 | tf_op jit(solution)/shard_map/all_gather | solution.py:71
  9.5 134.1 %all-gather.13.cloned.1.call-start = ((), (), s32[]{:S(2)}) async-start(), calls=%async_computation.3 | async-start | bytes 2621440 | tf_op jit(solution)/shard_map/all_gather | solution.py:74
  10.1 157.1 %all-gather.15.cloned.1.call-start = ((), (), s32[]{:S(2)}) async-start(), calls=%async_computation.4 | async-start | bytes 10485760 | tf_op jit(solution)/shard_map/all_gather | solution.py:75
  10.7 216.2 %all-gather.17.cloned.1.call-start = ((), (), s32[]{:S(2)}) async-start(), calls=%async_computation.5 | async-start | bytes 10485760 | tf_op jit(solution)/shard_map/all_gather | solution.py:76
  11.3 448.7 %all-reduce.3.cloned.1.call-start = ((), (), s32[]{:S(2)}) async-start(), calls=%async_computation.6 | async-start | bytes 1048576 | tf_op jit(solution)/shard_map/psum | solution.py:294
  15.2 122.7 %copy-start.20 = (bf16[64,16,64]{2,1,0:T(8,128)(2,1)}, bf16[64,16,64]{2,1,0:T(8,128)(2,1)S(1)}, u32[]{:S(2)}) copy-start(bf16[64,16,64]{2,1,0:T(8,128)(2,1)S(1)} %reshape.437) | copy-start | bytes 393220
  16.0 116.4 %copy-start.38 = (pred[256,256]{0,1:T(8,128)(4,1)}, pred[256,256]{0,1:T(8,128)(4,1)S(1)}, u32[]{:S(2)}) copy-start(pred[256,256]{0,1:T(8,128)(4,1)S(1)} %get-tuple-element.30) | copy-start | bytes 196612
  16.0 120.8 %copy-start.36 = (pred[256,256]{0,1:T(8,128)(4,1)}, pred[256,256]{0,1:T(8,128)(4,1)S(1)}, u32[]{:S(2)}) copy-start(pred[256,256]{0,1:T(8,128)(4,1)S(1)} %get-tuple-element.33) | copy-start | bytes 196612
  16.0 124.7 %copy-start.33 = (pred[256,256]{0,1:T(8,128)(4,1)}, pred[256,256]{0,1:T(8,128)(4,1)S(1)}, u32[]{:S(2)}) copy-start(pred[256,256]{0,1:T(8,128)(4,1)S(1)} %get-tuple-element.32) | copy-start | bytes 196612
  37.5 48.9 %copy-start.14 = (bf16[256,1024]{0,1:T(8,128)(2,1)}, bf16[256,1024]{0,1:T(8,128)(2,1)S(1)}, u32[]{:S(2)}) copy-start(bf16[256,1024]{0,1:T(8,128)(2,1)S(1)} %copy.114) | copy-start | bytes 1572868
  37.5 49.8 %collective-permute-start.2 = (bf16[256,16,64]{0,2,1:T(8,128)(2,1)S(1)}, bf16[256,16,64]{0,2,1:T(8,128)(2,1)S(1)}, u32[]{:S(2)}, u32[]{:S(2)}) collective-permute-start(bf16[256,16,64]{0,2,1:T(8,128)(2,1)S(1)} %bitcast.309), channel_id=1, source_target_pairs={{1,0},{2,1},{3,2},{4,3},{5,4},{6,5},{7,6},{9,8},{10,9},{11,10},{12... | collective-permute-start | bytes 1572872 | tf_op jit(solution)/shard_map/ppermute | solution.py:16
  38.8 49.8 %collective-permute-start = (bf16[256,16,64]{0,2,1:T(8,128)(2,1)S(1)}, bf16[256,16,64]{0,2,1:T(8,128)(2,1)}, u32[]{:S(2)}, u32[]{:S(2)}) collective-permute-start(bf16[256,16,64]{0,2,1:T(8,128)(2,1)S(1)} %bitcast.310), channel_id=1, source_target_pairs={{0,1},{1,2},{2,3},{3,4},{4,5},{5,6},{6,7},{8,9},{9,10},{10,11},{11... | collective-permute-start | bytes 1572872 | tf_op jit(solution)/shard_map/ppermute | solution.py:16
  62.5 30.7 %collective-permute-start.3 = (bf16[256,16,64]{0,2,1:T(8,128)(2,1)}, bf16[256,16,64]{0,2,1:T(8,128)(2,1)}, u32[]{:S(2)}, u32[]{:S(2)}) collective-permute-start(bf16[256,16,64]{0,2,1:T(8,128)(2,1)} %bitcast.8), channel_id=1, source_target_pairs={{1,0},{2,1},{3,2},{4,3},{5,4},{6,5},{7,6},{9,8},{10,9},{11,10},{12... | collective-permute-start | bytes 1572872 | tf_op jit(solution)/shard_map/ppermute | solution.py:16
  63.8 30.8 %collective-permute-start.1 = (bf16[256,16,64]{0,2,1:T(8,128)(2,1)}, bf16[256,16,64]{0,2,1:T(8,128)(2,1)}, u32[]{:S(2)}, u32[]{:S(2)}) collective-permute-start(bf16[256,16,64]{0,2,1:T(8,128)(2,1)} %bitcast.8), channel_id=1, source_target_pairs={{0,1},{1,2},{2,3},{3,4},{4,5},{5,6},{6,7},{8,9},{9,10},{10,11},{11... | collective-permute-start | bytes 1572872 | tf_op jit(solution)/shard_map/ppermute | solution.py:16
  87.3 45.1 %copy-start.4 = (f32[16,256,256]{1,2,0:T(8,128)}, f32[16,256,256]{1,2,0:T(8,128)S(1)}, u32[]{:S(2)}) copy-start(f32[16,256,256]{1,2,0:T(8,128)S(1)} %get-tuple-element.46) | copy-start | bytes 12582916
  87.3 15.1 %copy-start.26 = (bf16[256,16,64]{0,2,1:T(8,128)(2,1)}, bf16[256,16,64]{0,2,1:T(8,128)(2,1)S(1)}, u32[]{:S(2)}) copy-start(bf16[256,16,64]{0,2,1:T(8,128)(2,1)S(1)} %collective-permute-done.2) | copy-start | bytes 1572868
  87.3 39.4 %collective-permute-start.6 = (bf16[256,16,64]{0,2,1:T(8,128)(2,1)S(1)}, bf16[256,16,64]{0,2,1:T(8,128)(2,1)S(1)}, u32[]{:S(2)}, u32[]{:S(2)}) collective-permute-start(bf16[256,16,64]{0,2,1:T(8,128)(2,1)S(1)} %collective-permute-done.2), channel_id=1, source_target_pairs={{1,0},{2,1},{3,2},{4,3},{5,4},{6,5},{7,6},{9,8},{10,9},{11,10},{12... | collective-permute-start | bytes 1572872 | tf_op jit(solution)/shard_map/ppermute | solution.py:16
  88.7 37.2 %collective-permute-start.4 = (bf16[256,16,64]{0,2,1:T(8,128)(2,1)}, bf16[256,16,64]{0,2,1:T(8,128)(2,1)S(1)}, u32[]{:S(2)}, u32[]{:S(2)}) collective-permute-start(bf16[256,16,64]{0,2,1:T(8,128)(2,1)} %collective-permute-done), channel_id=1, source_target_pairs={{0,1},{1,2},{2,3},{3,4},{4,5},{5,6},{6,7},{8,9},{9,10},{10,11},{11... | collective-permute-start | bytes 1572872 | tf_op jit(solution)/shard_map/ppermute | solution.py:16
  93.2 43.5 %collective-permute-start.7 = (bf16[256,16,64]{0,2,1:T(8,128)(2,1)}, bf16[256,16,64]{0,2,1:T(8,128)(2,1)S(1)}, u32[]{:S(2)}, u32[]{:S(2)}) collective-permute-start(bf16[256,16,64]{0,2,1:T(8,128)(2,1)} %collective-permute-done.3), channel_id=1, source_target_pairs={{1,0},{2,1},{3,2},{4,3},{5,4},{6,5},{7,6},{9,8},{10,9},{11,10},{12... | collective-permute-start | bytes 1572872 | tf_op jit(solution)/shard_map/ppermute | solution.py:16
  94.6 45.9 %collective-permute-start.5 = (bf16[256,16,64]{0,2,1:T(8,128)(2,1)}, bf16[256,16,64]{0,2,1:T(8,128)(2,1)S(1)}, u32[]{:S(2)}, u32[]{:S(2)}) collective-permute-start(bf16[256,16,64]{0,2,1:T(8,128)(2,1)} %collective-permute-done.1), channel_id=1, source_target_pairs={{0,1},{1,2},{2,3},{3,4},{4,5},{5,6},{6,7},{8,9},{9,10},{10,11},{11... | collective-permute-start | bytes 1572872 | tf_op jit(solution)/shard_map/ppermute | solution.py:16
  101.5 36.7 %copy-start = (f32[16,256,256]{1,2,0:T(8,128)}, f32[16,256,256]{1,2,0:T(8,128)S(1)}, u32[]{:S(2)}) copy-start(f32[16,256,256]{1,2,0:T(8,128)S(1)} %get-tuple-element.42) | copy-start | bytes 12582916
  102.4 32.2 %copy-start.2 = (f32[16,256,256]{1,2,0:T(8,128)}, f32[16,256,256]{1,2,0:T(8,128)S(1)}, u32[]{:S(2)}) copy-start(f32[16,256,256]{1,2,0:T(8,128)S(1)} %get-tuple-element.40) | copy-start | bytes 12582916
  126.7 14.0 %copy-start.6 = (f32[16,256,256]{1,2,0:T(8,128)}, f32[16,256,256]{1,2,0:T(8,128)S(1)}, u32[]{:S(2)}) copy-start(f32[16,256,256]{1,2,0:T(8,128)S(1)} %get-tuple-element.38) | copy-start | bytes 12582916
  143.6 23.6 %copy-start.48 = (f32[4096]{0:T(1024)S(1)}, f32[4096]{0:T(1024)}, u32[]{:S(2)}) copy-start(f32[4096]{0:T(1024)} %convert_element_type.252) | copy-start | bytes 49156
  143.6 23.6 %copy-start.58 = (f32[1024]{0:T(1024)S(1)}, f32[1024]{0:T(1024)}, u32[]{:S(2)}) copy-start(f32[1024]{0:T(1024)} %convert_element_type.249) | copy-start | bytes 12292
  143.6 23.6 %copy-start.59 = (f32[1024]{0:T(1024)S(1)}, f32[1024]{0:T(1024)}, u32[]{:S(2)}) copy-start(f32[1024]{0:T(1024)} %convert_element_type.250) | copy-start | bytes 12292
  146.4 20.8 %copy-start.49 = (f32[256]{0:T(256)}, f32[256]{0:T(256)S(1)}, u32[]{:S(2)}) copy-start(f32[256]{0:T(256)S(1)} %broadcast_multiply_fusion.1) | copy-start | bytes 3076
  146.6 20.6 %copy-start.51 = (f32[256]{0:T(256)}, f32[256]{0:T(256)S(1)}, u32[]{:S(2)}) copy-start(f32[256]{0:T(256)S(1)} %multiply_reduce_fusion.3) | copy-start | bytes 3076
  146.6 20.5 %copy-start.55 = (f32[256]{0:T(256)}, f32[256]{0:T(256)S(1)}, u32[]{:S(2)}) copy-start(f32[256]{0:T(256)S(1)} %fusion.210) | copy-start | bytes 3076
  175.0 66.2 %copy-start.25 = (bf16[1,256,1024]{2,1,0:T(8,128)(2,1)S(1)}, bf16[1,256,1024]{2,1,0:T(8,128)(2,1)}, u32[]{:S(2)}) copy-start(bf16[1,256,1024]{2,1,0:T(8,128)(2,1)} %param.21) | copy-start | bytes 1572868
  226.9 14.3 %copy-start.46 = (f32[1024]{0:T(1024)S(1)}, f32[1024]{0:T(1024)}, u32[]{:S(2)}) copy-start(f32[1024]{0:T(1024)} %convert_element_type.255) | copy-start | bytes 12292
  226.9 15.3 %copy-start.47 = (f32[1024]{0:T(1024)S(1)}, f32[1024]{0:T(1024)}, u32[]{:S(2)}) copy-start(f32[1024]{0:T(1024)} %convert_element_type.256) | copy-start | bytes 12292
  299.5 16.6 %copy-start.15 = (bf16[256,1024]{0,1:T(8,128)(2,1)S(1)}, bf16[256,1024]{0,1:T(8,128)(2,1)}, u32[]{:S(2)}) copy-start(bf16[256,1024]{0,1:T(8,128)(2,1)} %copy-done.14) | copy-start | bytes 1572868
  300.9 15.7 %copy-start.13 = (bf16[16,256,64]{1,2,0:T(8,128)(2,1)S(1)}, bf16[16,256,64]{1,2,0:T(8,128)(2,1)}, u32[]{:S(2)}) copy-start(bf16[16,256,64]{1,2,0:T(8,128)(2,1)} %fusion.152) | copy-start | bytes 1572868
  302.5 28.7 %collective-permute-start.8 = (bf16[256,16,64]{0,2,1:T(8,128)(2,1)}, bf16[256,16,64]{0,2,1:T(8,128)(2,1)}, u32[]{:S(2)}, u32[]{:S(2)}) collective-permute-start(bf16[256,16,64]{0,2,1:T(8,128)(2,1)} %fusion.167), channel_id=1, source_target_pairs={{1,0},{2,1},{3,2},{4,3},{5,4},{6,5},{7,6},{9,8},{10,9},{11,10},{12... | collective-permute-start | bytes 1572872 | tf_op jit(solution)/shard_map/ppermute | solution.py:16
  303.8 44.5 %collective-permute-start.12 = (bf16[256,16,64]{0,2,1:T(8,128)(2,1)}, bf16[256,16,64]{0,2,1:T(8,128)(2,1)}, u32[]{:S(2)}, u32[]{:S(2)}) collective-permute-start(bf16[256,16,64]{0,2,1:T(8,128)(2,1)} %fusion.171), channel_id=1, source_target_pairs={{1,0},{2,1},{3,2},{4,3},{5,4},{6,5},{7,6},{9,8},{10,9},{11,10},{12... | collective-permute-start | bytes 1572872 | tf_op jit(solution)/shard_map/ppermute | solution.py:16
  305.1 37.0 %collective-permute-start.10 = (bf16[256,16,64]{0,2,1:T(8,128)(2,1)}, bf16[256,16,64]{0,2,1:T(8,128)(2,1)}, u32[]{:S(2)}, u32[]{:S(2)}) collective-permute-start(bf16[256,16,64]{0,2,1:T(8,128)(2,1)} %fusion.166), channel_id=1, source_target_pairs={{0,1},{1,2},{2,3},{3,4},{4,5},{5,6},{6,7},{8,9},{9,10},{10,11},{11... | collective-permute-start | bytes 1572872 | tf_op jit(solution)/shard_map/ppermute | solution.py:16
  311.0 54.1 %collective-permute-start.14 = (bf16[256,16,64]{0,2,1:T(8,128)(2,1)}, bf16[256,16,64]{0,2,1:T(8,128)(2,1)}, u32[]{:S(2)}, u32[]{:S(2)}) collective-permute-start(bf16[256,16,64]{0,2,1:T(8,128)(2,1)} %fusion.168), channel_id=1, source_target_pairs={{0,1},{1,2},{2,3},{3,4},{4,5},{5,6},{6,7},{8,9},{9,10},{10,11},{11... | collective-permute-start | bytes 1572872 | tf_op jit(solution)/shard_map/ppermute | solution.py:16
  331.2 17.1 %copy-start.1 = (f32[16,256,256]{1,2,0:T(8,128)S(1)}, f32[16,256,256]{1,2,0:T(8,128)}, u32[]{:S(2)}) copy-start(f32[16,256,256]{1,2,0:T(8,128)} %copy-done) | copy-start | bytes 12582916
  333.2 38.7 %collective-permute-start.9 = (bf16[256,16,64]{0,2,1:T(8,128)(2,1)S(1)}, bf16[256,16,64]{0,2,1:T(8,128)(2,1)S(1)}, u32[]{:S(2)}, u32[]{:S(2)}) collective-permute-start(bf16[256,16,64]{0,2,1:T(8,128)(2,1)S(1)} %add_convert_fusion.11), channel_id=1, source_target_pairs={{1,0},{2,1},{3,2},{4,3},{5,4},{6,5},{7,6},{9,8},{10,9},{11,10},{12... | collective-permute-start | bytes 1572872 | tf_op jit(solution)/shard_map/ppermute | solution.py:16
  343.9 43.7 %collective-permute-start.11 = (bf16[256,16,64]{0,2,1:T(8,128)(2,1)S(1)}, bf16[256,16,64]{0,2,1:T(8,128)(2,1)S(1)}, u32[]{:S(2)}, u32[]{:S(2)}) collective-permute-start(bf16[256,16,64]{0,2,1:T(8,128)(2,1)S(1)} %add_convert_fusion.10), channel_id=1, source_target_pairs={{0,1},{1,2},{2,3},{3,4},{4,5},{5,6},{6,7},{8,9},{9,10},{10,11},{11... | collective-permute-start | bytes 1572872 | tf_op jit(solution)/shard_map/ppermute | solution.py:16
  350.5 37.4 %copy-start.24 = (bf16[1024,1024]{1,0:T(8,128)(2,1)S(1)}, bf16[1024,1024]{1,0:T(8,128)(2,1)}, u32[]{:S(2)}) copy-start(bf16[1024,1024]{1,0:T(8,128)(2,1)} %all-gather.9.cloned.1.call-done) | copy-start | bytes 6291460
  350.5 38.2 %collective-permute-start.13 = (bf16[256,16,64]{0,2,1:T(8,128)(2,1)S(1)}, bf16[256,16,64]{0,2,1:T(8,128)(2,1)S(1)}, u32[]{:S(2)}, u32[]{:S(2)}) collective-permute-start(bf16[256,16,64]{0,2,1:T(8,128)(2,1)S(1)} %add_convert_fusion.8), channel_id=1, source_target_pairs={{1,0},{2,1},{3,2},{4,3},{5,4},{6,5},{7,6},{9,8},{10,9},{11,10},{12... | collective-permute-start | bytes 1572872 | tf_op jit(solution)/shard_map/ppermute | solution.py:16
  367.3 31.4 %copy-start.32 = (f32[256,16,64]{0,2,1:T(8,128)S(1)}, f32[256,16,64]{0,2,1:T(8,128)}, u32[]{:S(2)}) copy-start(f32[256,16,64]{0,2,1:T(8,128)} %fusion.104) | copy-start | bytes 3145732
  367.3 31.4 %collective-permute-start.15 = (bf16[256,16,64]{0,2,1:T(8,128)(2,1)S(1)}, bf16[256,16,64]{0,2,1:T(8,128)(2,1)S(1)}, u32[]{:S(2)}, u32[]{:S(2)}) collective-permute-start(bf16[256,16,64]{0,2,1:T(8,128)(2,1)S(1)} %add_convert_fusion.7), channel_id=1, source_target_pairs={{0,1},{1,2},{2,3},{3,4},{4,5},{5,6},{6,7},{8,9},{9,10},{10,11},{11... | collective-permute-start | bytes 1572872 | tf_op jit(solution)/shard_map/ppermute | solution.py:16
  (47 other events, 191.8 us)
Sparse Core Ops, SparseCore 0:
  9.7 25.2 all-gather.8
  36.6 22.5 all-gather.10
  60.8 22.5 all-gather.6
  84.8 22.5 all-gather.12
  108.8 58.2 all-gather.14
  168.6 58.2 all-gather.16
  318.0 141.9 all-reduce.2
where the time goes:
time: 476 us; the launch traced here: 470 us
  waiting for transfers between devices  254 us (53%)
  matrix products  123 us (26%)
  starting transfers between devices  51 us (11%)
  between operations  15.7 us (3%)
  other arithmetic  14.2 us (3%)
  local copies, waits for them, and re-layouts  12.6 us (3%)
    ppermute x16, waiting for transfers between devices, shifted(): return lax.ppermute(block, axis, route)  70.1 us
    psum x1, waiting for transfers between devices, per_device(): lax.psum((grad_pkey.reshape(prefix_count, width_model), grad_pvalue.resha...  59.4 us
    all_gather x1, waiting for transfers between devices, per_device(): lax.all_gather(w_down, 'row', axis=0, tiled=True)  51.9 us
    ppermute x16, starting transfers between devices, shifted(): return lax.ppermute(block, axis, route)  50.8 us
    dot_general x1, matrix products, per_device(): jnp.dot(grad_pre, full_up.T, preferred_element_type=jnp.float32)  24.5 us
    all_gather x1, waiting for transfers between devices, per_device(): lax.all_gather(w_up, 'row', axis=0, tiled=True)  20.5 us
    all_gather x1, waiting for transfers between devices, per_device(): lax.all_gather(w_key, 'row', axis=0, tiled=True)  19 us
    dot_general x6, matrix products, grad_probs_of(): jnp.einsum('qhd,khd->hqk', grad_attended, value_block, preferred_element_...  15.2 us
  transfers between devices with their start and end apart: 23, of which 11 were waited for; matrix products, arithmetic and copies ran while one was open for 15% of the time, Pallas kernels for 0%

commit v1 on v0

--- a/solution.py
+++ b/solution.py
@@ -8,6 +8,27 @@
 REACH = 2
 ln_eps = 1e-05
 masked_fill = -1e30
+
+
+def in_order(blocks, dim):
+    shape = list(blocks.shape[1:])
+    shape[dim] *= blocks.shape[0]
+    return jnp.moveaxis(blocks, 0, dim).reshape(shape)
+
+
+def collected_by_bits(x, axis):
+    size, mine = (lax.axis_size(axis), lax.axis_index(axis))
+    pieces, bit = (x[None], 1)
+    while bit < size:
+        theirs = lax.ppermute(pieces, axis, [(i, i ^ bit) for i in range(size)])
+        low = mine & bit == 0
+        pieces = jnp.concatenate([jnp.where(low, pieces, theirs), jnp.where(low, theirs, pieces)])
+        bit *= 2
+    return pieces
+
+
+def doubled_up(shard, axis, dim):
+    return in_order(collected_by_bits(shard, axis), dim)
 
 
 def shifted(block, axis, distance):
@@ -72,7 +93,7 @@
         lax.all_gather(w_key, "row", axis=0, tiled=True),
         lax.all_gather(w_value, "row", axis=0, tiled=True),
         lax.all_gather(w_out, "row", axis=0, tiled=True),
-        lax.all_gather(w_up, "row", axis=0, tiled=True),
+        doubled_up(w_up, "row", 0),
         lax.all_gather(w_down, "row", axis=0, tiled=True),
     )
     full_query, full_key, full_value, full_out, full_up, full_down = gathered

time: 476 us -> 459 us (0.964)
  waiting for transfers between devices: 254 us -> 215 us
  other arithmetic: 14.2 us -> 31 us
    all_gather x1, waiting for transfers between devices: 51.9 us -> 11.1 us  [per_device(): lax.all_gather(w_down, 'row', axis=0, tiled=True)]
    all_gather x1 -> x0, waiting for transfers between devices: 20.5 us -> none  [per_device(): lax.all_gather(w_up, 'row', axis=0, tiled=True)]
    all_gather x1, waiting for transfers between devices: 14.3 us -> 25.6 us  [per_device(): lax.all_gather(w_query, 'row', axis=0, tiled=True)]
    all_gather x1, waiting for transfers between devices: 15 us -> 25.7 us  [per_device(): lax.all_gather(w_value, 'row', axis=0, tiled=True)]
    concatenate x0 -> x2, other arithmetic: none -> 9.75 us  [collected_by_bits(): jnp.concatenate([jnp.where(low, pieces, theirs), jnp.where(low, theirs, p...]
    select_n x0 -> x2, other arithmetic: none -> 7.04 us  [collected_by_bits(): jnp.where(low, pieces, theirs)]
  transfers between devices with their start and end apart: 23 -> 24, of which waited for: 11 -> 10; matrix products, arithmetic and copies ran while one was open for 15% -> 19% of each run, Pallas kernels for 0% -> 0%
where the time goes in v1:
time: 459 us; the launch traced here: 453 us
  waiting for transfers between devices  215 us (47%)
  matrix products  123 us (27%)
  starting transfers between devices  54.4 us (12%)
  other arithmetic  31 us (7%)
  between operations  16 us (3%)
  local copies, waits for them, and re-layouts  13.8 us (3%)
    ppermute x16, waiting for transfers between devices, shifted(): return lax.ppermute(block, axis, route)  70 us
    psum x1, waiting for transfers between devices, per_device(): lax.psum((grad_pkey.reshape(prefix_count, width_model), grad_pvalue.resha...  59.4 us
    ppermute x16, starting transfers between devices, shifted(): return lax.ppermute(block, axis, route)  50.9 us
    all_gather x1, waiting for transfers between devices, per_device(): lax.all_gather(w_value, 'row', axis=0, tiled=True)  25.7 us
    all_gather x1, waiting for transfers between devices, per_device(): lax.all_gather(w_query, 'row', axis=0, tiled=True)  25.6 us
    dot_general x1, matrix products, per_device(): jnp.dot(grad_pre, full_up.T, preferred_element_type=jnp.float32)  24.4 us
    all_gather x1, waiting for transfers between devices, per_device(): lax.all_gather(w_key, 'row', axis=0, tiled=True)  20.2 us
    dot_general x6, matrix products, grad_probs_of(): jnp.einsum('qhd,khd->hqk', grad_attended, value_block, preferred_element_...  15.2 us
  transfers between devices with their start and end apart: 24, of which 10 were waited for; matrix products, arithmetic and copies ran while one was open for 19% of the time, Pallas kernels for 0%

profile of v1, /device:TPU:0, one launch (start us, length us, event | category | flops | bytes accessed | tf_op | source)
XLA Modules:
  0.0 453.0 jit_solution(714060359155132854)
XLA Ops:
  15.5 1.9 broadcast_select_fusion.3
  17.4 2.3 pad_maximum_fusion.1
  20.8 2.8 collective-permute-start.9
  23.6 20.2 %all-gather.8.cloned.1.call-done = bf16[1024,1024]{1,0:T(8,128)(2,1)} async-done(((bf16[256,1024]{1,0:T(8,128)(2,1)}), bf16[1024,1024]{1,0:T(8,128)(2,1)}) %all-gather.8.cloned.1.call-update) | async-done | bytes 2097168 | tf_op jit(solution)/shard_map/all_gather | solution.py:93
  43.8 2.3 convolution_convert_fusion.1
  47.6 5.3 %collective-permute-start = (bf16[256,16,64]{0,2,1:T(8,128)(2,1)S(1)}, bf16[256,16,64]{0,2,1:T(8,128)(2,1)}, u32[]{:S(2)}, u32[]{:S(2)}) collective-permute-start(bf16[256,16,64]{0,2,1:T(8,128)(2,1)S(1)} %bitcast.316), channel_id=1, source_target_pairs={{0,1},{1,2},{2,3},{3,4},{4,5},{5,6},{6,7},{8,9},{9,10},{10,11},{11... | collective-permute-start | bytes 1572872 | tf_op jit(solution)/shard_map/ppermute | solution.py:37
  53.0 25.7 %all-gather.10.cloned.1.call-done = bf16[1024,1024]{1,0:T(8,128)(2,1)} async-done(((bf16[256,1024]{1,0:T(8,128)(2,1)}), bf16[1024,1024]{1,0:T(8,128)(2,1)}) %all-gather.10.cloned.1.call-update) | async-done | bytes 2097168 | tf_op jit(solution)/shard_map/all_gather | solution.py:94
  78.7 2.3 fusion.154
  83.3 5.4 %collective-permute-start.1 = (bf16[256,16,64]{0,2,1:T(8,128)(2,1)}, bf16[256,16,64]{0,2,1:T(8,128)(2,1)}, u32[]{:S(2)}, u32[]{:S(2)}) collective-permute-start(bf16[256,16,64]{0,2,1:T(8,128)(2,1)} %bitcast.8), channel_id=1, source_target_pairs={{0,1},{1,2},{2,3},{3,4},{4,5},{5,6},{6,7},{8,9},{9,10},{10,11},{11... | collective-permute-start | bytes 1572872 | tf_op jit(solution)/shard_map/ppermute | solution.py:37
  88.7 25.6 %all-gather.6.cloned.1.call-done = bf16[1024,1024]{1,0:T(8,128)(2,1)} async-done(((bf16[256,1024]{1,0:T(8,128)(2,1)}), bf16[1024,1024]{1,0:T(8,128)(2,1)}) %all-gather.6.cloned.1.call-update) | async-done | bytes 2097168 | tf_op jit(solution)/shard_map/all_gather | solution.py:92
  114.3 2.3 fusion.153
  119.5 4.6 %collective-permute-start.4 = (bf16[256,16,64]{0,2,1:T(8,128)(2,1)}, bf16[256,16,64]{0,2,1:T(8,128)(2,1)S(1)}, u32[]{:S(2)}, u32[]{:S(2)}) collective-permute-start(bf16[256,16,64]{0,2,1:T(8,128)(2,1)} %collective-permute-done), channel_id=1, source_target_pairs={{0,1},{1,2},{2,3},{3,4},{4,5},{5,6},{6,7},{8,9},{9,10},{10,11},{11... | collective-permute-start | bytes 1572872 | tf_op jit(solution)/shard_map/ppermute | solution.py:37
  125.4 5.1 %collective-permute-start.5 = (bf16[256,16,64]{0,2,1:T(8,128)(2,1)}, bf16[256,16,64]{0,2,1:T(8,128)(2,1)S(1)}, u32[]{:S(2)}, u32[]{:S(2)}) collective-permute-start(bf16[256,16,64]{0,2,1:T(8,128)(2,1)} %collective-permute-done.1), channel_id=1, source_target_pairs={{0,1},{1,2},{2,3},{3,4},{4,5},{5,6},{6,7},{8,9},{9,10},{10,11},{11... | collective-permute-start | bytes 1572872 | tf_op jit(solution)/shard_map/ppermute | solution.py:37
  133.3 23.4 %collective-permute-done.4 = bf16[256,16,64]{0,2,1:T(8,128)(2,1)S(1)} collective-permute-done((bf16[256,16,64]{0,2,1:T(8,128)(2,1)}, bf16[256,16,64]{0,2,1:T(8,128)(2,1)S(1)}, u32[]{:S(2)}, u32[]{:S(2)}) %collective-permute-start.4) | collective-permute-done | bytes 524320 | tf_op jit(solution)/shard_map/ppermute | solution.py:37
  163.2 2.2 fusion.89
  165.5 2.1 fusion.95
  169.1 2.3 fusion.145
  172.2 2.3 fusion.248
  174.5 2.9 fusion.249
  177.8 5.1 %broadcast_select_fusion.1 = (bf16[2,256,4096]{2,1,0:T(8,128)(2,1)}, bf16[2,256,4096]{2,1,0:T(8,128)(2,1)}) fusion(bf16[2,256,4096]{2,1,0:T(8,128)(2,1)} %collective-permute-done.9, pred[]{:T(512)S(6)} %eq.57, bf16[1,256,4096]{2,1,0:T(8,128)(2,1)S(1)} %copy-done.5, bf16[1,256,4096]{2,1,0:T(8,128)(2,1)S(1)} %copy-done.3), kind=kLoop, calls=%fused_computation.41 | loop fusion | flops 6291456 | bytes 16777216 | tf_op jit(solution)/shard_map/jit(_where)/select_n | solution.py:25
  182.9 7.5 %pad_maximum_fusion = bf16[4,256,4096]{2,1,0:T(8,128)(2,1)} fusion(bf16[2,256,4096]{2,1,0:T(8,128)(2,1)} %get-tuple-element.27, bf16[2,256,4096]{2,1,0:T(8,128)(2,1)} %get-tuple-element.26), kind=kLoop, calls=%fused_computation | loop fusion | flops 4194304 | bytes 16777216 | tf_op jit(solution)/shard_map/concatenate | solution.py:25
  190.4 7.9 %convolution_add_fusion = f32[256,4096]{1,0:T(8,128)} fusion(bf16[1024,4096]{1,0:T(8,128)(2,1)} %bitcast.301, f32[4096]{0:T(1024)S(1)} %copy-done.53, f32[256,1024]{1,0:T(8,128)S(1)} %get-tuple-element.54, f32[1024]{0:T(1024)S(1)} %copy-done.64, f32[1024]{0:T(1024)S(1)} %copy-done.63, f32[256]{0:T(256)S(1)} %fusion.210, f32[256]{0:T(256)S(1)} %broadcast_multiply_fusion.1), kind=kOutput, calls=%fused_computation.2 | convolution fusion | flops 2149842944 | bytes 13658112 | tf_op jit(solution)/shard_map/dot_general | solution.py:195
  198.3 11.1 %all-gather.14.cloned.1.call-done = bf16[4096,1024]{1,0:T(8,128)(2,1)} async-done(((bf16[1024,1024]{1,0:T(8,128)(2,1)}), bf16[4096,1024]{1,0:T(8,128)(2,1)}) %all-gather.14.cloned.1.call-update) | async-done | bytes 8388624 | tf_op jit(solution)/shard_map/all_gather | solution.py:97
  209.4 14.3 %fusion.250 = (f32[256]{0:T(256)S(1)}, f32[256,1024]{1,0:T(8,128)S(1)}) fusion(f32[1024]{0:T(1024)} %convert_element_type.254, bf16[4096,1024]{1,0:T(8,128)(2,1)} %all-gather.14.cloned.1.call-done, f32[256,4096]{1,0:T(8,128)} %convolution_add_fusion, f32[1024]{0:T(1024)} %convert_element_type.250, f32[1024]{0:T(1024)} %convert_element_type.249, ...), kind=kOutput, calls=%fused_computation.312 | convolution fusion | flops 2217475840 | bytes 14695424 | tf_op jit(solution)/shard_map/dot_general | solution.py:201
  226.5 24.4 %multiply_reduce_fusion.1 = (f32[256]{0:T(256)}, f32[256,1024]{1,0:T(8,128)}) fusion(f32[256,1024]{1,0:T(8,128)S(1)} %get-tuple-element.54, f32[256]{0:T(256)} %copy-done.54, f32[1024]{0:T(1024)} %convert_element_type.249, bf16[1024,4096]{1,0:T(8,128)(2,1)} %bitcast.302, f32[256,4096]{1,0:T(8,128)} %convolution_add_fusion, ...), kind=kOutput, calls=%fused_computation.201 | convolution fusion | flops 4376231936 | bytes 24655872 | tf_op jit(solution)/shard_map/dot_general | solution.py:215
  254.2 2.3 convolution_convert_fusion
  257.9 4.3 fusion.168
  264.6 2.1 fusion.104
  268.0 2.5 multiply_convert_fusion.4
  270.5 1.9 copy.145
  272.4 2.1 convolution_multiply_fusion.6
  274.5 1.9 copy.144
  276.5 3.8 multiply_convert_fusion
  287.5 6.0 %collective-permute-start.12 = (bf16[256,16,64]{0,2,1:T(8,128)(2,1)}, bf16[256,16,64]{0,2,1:T(8,128)(2,1)}, u32[]{:S(2)}, u32[]{:S(2)}) collective-permute-start(bf16[256,16,64]{0,2,1:T(8,128)(2,1)} %fusion.166), channel_id=1, source_target_pairs={{0,1},{1,2},{2,3},{3,4},{4,5},{5,6},{6,7},{8,9},{9,10},{10,11},{11... | collective-permute-start | bytes 1572872 | tf_op jit(solution)/shard_map/ppermute | solution.py:37
  293.5 5.0 %collective-permute-start.16 = (bf16[256,16,64]{0,2,1:T(8,128)(2,1)}, bf16[256,16,64]{0,2,1:T(8,128)(2,1)}, u32[]{:S(2)}, u32[]{:S(2)}) collective-permute-start(bf16[256,16,64]{0,2,1:T(8,128)(2,1)} %fusion.168), channel_id=1, source_target_pairs={{0,1},{1,2},{2,3},{3,4},{4,5},{5,6},{6,7},{8,9},{9,10},{10,11},{11... | collective-permute-start | bytes 1572872 | tf_op jit(solution)/shard_map/ppermute | solution.py:37
  300.4 2.2 convolution_bitcast_fusion
  302.6 3.8 multiply_convert_fusion.3
  306.5 2.6 multiply_convert_fusion.2
  313.7 2.0 add_convert_fusion.11
  316.9 7.6 %collective-permute-done.12 = bf16[256,16,64]{0,2,1:T(8,128)(2,1)} collective-permute-done((bf16[256,16,64]{0,2,1:T(8,128)(2,1)}, bf16[256,16,64]{0,2,1:T(8,128)(2,1)}, u32[]{:S(2)}, u32[]{:S(2)}) %collective-permute-start.12) | collective-permute-done | bytes 524320 | tf_op jit(solution)/shard_map/ppermute | solution.py:37
  326.3 4.4 collective-permute-start.13
  330.8 2.2 add_convert_fusion.8
  334.4 13.2 %collective-permute-done.16 = bf16[256,16,64]{0,2,1:T(8,128)(2,1)} collective-permute-done((bf16[256,16,64]{0,2,1:T(8,128)(2,1)}, bf16[256,16,64]{0,2,1:T(8,128)(2,1)}, u32[]{:S(2)}, u32[]{:S(2)}) %collective-permute-start.16) | collective-permute-done | bytes 524320 | tf_op jit(solution)/shard_map/ppermute | solution.py:37
  347.5 2.2 add_convert_fusion.7
  349.7 4.6 %collective-permute-start.17 = (bf16[256,16,64]{0,2,1:T(8,128)(2,1)S(1)}, bf16[256,16,64]{0,2,1:T(8,128)(2,1)S(1)}, u32[]{:S(2)}, u32[]{:S(2)}) collective-permute-start(bf16[256,16,64]{0,2,1:T(8,128)(2,1)S(1)} %add_convert_fusion.7), channel_id=1, source_target_pairs={{0,1},{1,2},{2,3},{3,4},{4,5},{5,6},{6,7},{8,9},{9,10},{10,11},{11... | collective-permute-start | bytes 1572872 | tf_op jit(solution)/shard_map/ppermute | solution.py:37
  354.3 15.7 %collective-permute-done.13 = bf16[256,16,64]{0,2,1:T(8,128)(2,1)S(1)} collective-permute-done((bf16[256,16,64]{0,2,1:T(8,128)(2,1)S(1)}, bf16[256,16,64]{0,2,1:T(8,128)(2,1)S(1)}, u32[]{:S(2)}, u32[]{:S(2)}) %collective-permute-start.13) | collective-permute-done | bytes 524320 | tf_op jit(solution)/shard_map/ppermute | solution.py:37
  371.1 10.1 %collective-permute-done.17 = bf16[256,16,64]{0,2,1:T(8,128)(2,1)S(1)} collective-permute-done((bf16[256,16,64]{0,2,1:T(8,128)(2,1)S(1)}, bf16[256,16,64]{0,2,1:T(8,128)(2,1)S(1)}, u32[]{:S(2)}, u32[]{:S(2)}) %collective-permute-start.17) | collective-permute-done | bytes 524320 | tf_op jit(solution)/shard_map/ppermute | solution.py:37
  383.0 59.4 %all-reduce.3.cloned.1.call-done = (f32[64,1024]{1,0:T(8,128)}, f32[64,1024]{1,0:T(8,128)}) async-done(((f32[64,1024]{1,0:T(8,128)}, f32[64,1024]{1,0:T(8,128)}), (f32[64,1024]{1,0:T(8,128)}, f32[64,1024]{1,0:T(8,128)})) %all-reduce.3.cloned.1.call-update) | async-done | bytes 524304 | tf_op jit(solution)/shard_map/psum | solution.py:315
  (264 shorter events, 63.9 us)
Async XLA Ops:
  7.2 8.3 %copy-start.30 = (bf16[256,4096]{1,0:T(8,128)(2,1)S(1)}, bf16[256,4096]{1,0:T(8,128)(2,1)}, u32[]{:S(2)}) copy-start(bf16[256,4096]{1,0:T(8,128)(2,1)} %param.34) | copy-start | bytes 6291460
  7.3 36.5 %all-gather.8.cloned.1.call-start = ((), (), s32[]{:S(2)}) async-start(), calls=%async_computation.1 | async-start | bytes 2621440 | tf_op jit(solution)/shard_map/all_gather | solution.py:93
  8.0 70.7 %all-gather.10.cloned.1.call-start = ((), (), s32[]{:S(2)}) async-start(), calls=%async_computation.2 | async-start | bytes 2621440 | tf_op jit(solution)/shard_map/all_gather | solution.py:94
  8.8 105.5 %all-gather.6.cloned.1.call-start = ((), (), s32[]{:S(2)}) async-start(), calls=%async_computation | async-start | bytes 2621440 | tf_op jit(solution)/shard_map/all_gather | solution.py:92
  9.5 165.0 %all-gather.12.cloned.1.call-start = ((), (), s32[]{:S(2)}) async-start(), calls=%async_computation.3 | async-start | bytes 2621440 | tf_op jit(solution)/shard_map/all_gather | solution.py:95
  10.1 199.3 %all-gather.14.cloned.1.call-start = ((), (), s32[]{:S(2)}) async-start(), calls=%async_computation.4 | async-start | bytes 10485760 | tf_op jit(solution)/shard_map/all_gather | solution.py:97
  10.1 5.3 %collective-permute-start.8 = (bf16[1,256,4096]{2,1,0:T(8,128)(2,1)}, bf16[1,256,4096]{2,1,0:T(8,128)(2,1)}, u32[]{:S(2)}, u32[]{:S(2)}) collective-permute-start(bf16[1,256,4096]{2,1,0:T(8,128)(2,1)} %bitcast.325), channel_id=1, source_target_pairs={{0,8},{8,0},{16,24},{24,16},{1,9},{9,1},{17,25},{25,17},{2,10},{10... | collective-permute-start | bytes 6291464 | tf_op jit(solution)/shard_map/ppermute | solution.py:23
  10.7 431.6 %all-reduce.3.cloned.1.call-start = ((), (), s32[]{:S(2)}) async-start(), calls=%async_computation.5 | async-start | bytes 1048576 | tf_op jit(solution)/shard_map/psum | solution.py:315
  14.8 153.9 %copy-start.24 = (bf16[64,16,64]{2,1,0:T(8,128)(2,1)}, bf16[64,16,64]{2,1,0:T(8,128)(2,1)S(1)}, u32[]{:S(2)}) copy-start(bf16[64,16,64]{2,1,0:T(8,128)(2,1)S(1)} %reshape.440) | copy-start | bytes 393220
  15.4 147.8 %copy-start.43 = (pred[256,256]{0,1:T(8,128)(4,1)}, pred[256,256]{0,1:T(8,128)(4,1)S(1)}, u32[]{:S(2)}) copy-start(pred[256,256]{0,1:T(8,128)(4,1)S(1)} %get-tuple-element.34) | copy-start | bytes 196612
  15.4 152.2 %copy-start.41 = (pred[256,256]{0,1:T(8,128)(4,1)}, pred[256,256]{0,1:T(8,128)(4,1)S(1)}, u32[]{:S(2)}) copy-start(pred[256,256]{0,1:T(8,128)(4,1)S(1)} %get-tuple-element.37) | copy-start | bytes 196612
  15.4 156.4 %copy-start.38 = (pred[256,256]{0,1:T(8,128)(4,1)}, pred[256,256]{0,1:T(8,128)(4,1)S(1)}, u32[]{:S(2)}) copy-start(pred[256,256]{0,1:T(8,128)(4,1)S(1)} %get-tuple-element.36) | copy-start | bytes 196612
  17.4 26.4 %copy-start.45 = (bf16[1,256,1024]{2,1,0:T(8,128)(2,1)S(1)}, bf16[1,256,1024]{2,1,0:T(8,128)(2,1)}, u32[]{:S(2)}) copy-start(bf16[1,256,1024]{2,1,0:T(8,128)(2,1)} %param.20) | copy-start | bytes 1572868
  20.8 156.9 %collective-permute-start.9 = (bf16[2,256,4096]{2,1,0:T(8,128)(2,1)}, bf16[2,256,4096]{2,1,0:T(8,128)(2,1)}, u32[]{:S(2)}, u32[]{:S(2)}) collective-permute-start(bf16[2,256,4096]{2,1,0:T(8,128)(2,1)} %pad_maximum_fusion.1), channel_id=1, source_target_pairs={{0,16},{8,24},{16,0},{24,8},{1,17},{9,25},{17,1},{25,9},{2,18},{10... | collective-permute-start | bytes 12582920 | tf_op jit(solution)/shard_map/ppermute | solution.py:23
  46.3 71.0 %copy-start.18 = (bf16[256,1024]{0,1:T(8,128)(2,1)}, bf16[256,1024]{0,1:T(8,128)(2,1)S(1)}, u32[]{:S(2)}) copy-start(bf16[256,1024]{0,1:T(8,128)(2,1)S(1)} %copy.114) | copy-start | bytes 1572868
  46.3 71.8 %collective-permute-start.2 = (bf16[256,16,64]{0,2,1:T(8,128)(2,1)S(1)}, bf16[256,16,64]{0,2,1:T(8,128)(2,1)S(1)}, u32[]{:S(2)}, u32[]{:S(2)}) collective-permute-start(bf16[256,16,64]{0,2,1:T(8,128)(2,1)S(1)} %bitcast.315), channel_id=1, source_target_pairs={{1,0},{2,1},{3,2},{4,3},{5,4},{6,5},{7,6},{9,8},{10,9},{11,10},{12... | collective-permute-start | bytes 1572872 | tf_op jit(solution)/shard_map/ppermute | solution.py:37
  47.6 71.9 %collective-permute-start = (bf16[256,16,64]{0,2,1:T(8,128)(2,1)S(1)}, bf16[256,16,64]{0,2,1:T(8,128)(2,1)}, u32[]{:S(2)}, u32[]{:S(2)}) collective-permute-start(bf16[256,16,64]{0,2,1:T(8,128)(2,1)S(1)} %bitcast.316), channel_id=1, source_target_pairs={{0,1},{1,2},{2,3},{3,4},{4,5},{5,6},{6,7},{8,9},{9,10},{10,11},{11... | collective-permute-start | bytes 1572872 | tf_op jit(solution)/shard_map/ppermute | solution.py:37
  82.0 42.1 %collective-permute-start.3 = (bf16[256,16,64]{0,2,1:T(8,128)(2,1)}, bf16[256,16,64]{0,2,1:T(8,128)(2,1)}, u32[]{:S(2)}, u32[]{:S(2)}) collective-permute-start(bf16[256,16,64]{0,2,1:T(8,128)(2,1)} %bitcast.8), channel_id=1, source_target_pairs={{1,0},{2,1},{3,2},{4,3},{5,4},{6,5},{7,6},{9,8},{10,9},{11,10},{12... | collective-permute-start | bytes 1572872 | tf_op jit(solution)/shard_map/ppermute | solution.py:37
  83.3 42.1 %collective-permute-start.1 = (bf16[256,16,64]{0,2,1:T(8,128)(2,1)}, bf16[256,16,64]{0,2,1:T(8,128)(2,1)}, u32[]{:S(2)}, u32[]{:S(2)}) collective-permute-start(bf16[256,16,64]{0,2,1:T(8,128)(2,1)} %bitcast.8), channel_id=1, source_target_pairs={{0,1},{1,2},{2,3},{3,4},{4,5},{5,6},{6,7},{8,9},{9,10},{10,11},{11... | collective-permute-start | bytes 1572872 | tf_op jit(solution)/shard_map/ppermute | solution.py:37
  118.2 45.1 %copy-start.8 = (f32[16,256,256]{1,2,0:T(8,128)}, f32[16,256,256]{1,2,0:T(8,128)S(1)}, u32[]{:S(2)}) copy-start(f32[16,256,256]{1,2,0:T(8,128)S(1)} %get-tuple-element.50) | copy-start | bytes 12582916
  118.2 15.1 %copy-start.31 = (bf16[256,16,64]{0,2,1:T(8,128)(2,1)}, bf16[256,16,64]{0,2,1:T(8,128)(2,1)S(1)}, u32[]{:S(2)}) copy-start(bf16[256,16,64]{0,2,1:T(8,128)(2,1)S(1)} %collective-permute-done.2) | copy-start | bytes 1572868
  118.2 39.4 %collective-permute-start.6 = (bf16[256,16,64]{0,2,1:T(8,128)(2,1)S(1)}, bf16[256,16,64]{0,2,1:T(8,128)(2,1)S(1)}, u32[]{:S(2)}, u32[]{:S(2)}) collective-permute-start(bf16[256,16,64]{0,2,1:T(8,128)(2,1)S(1)} %collective-permute-done.2), channel_id=1, source_target_pairs={{1,0},{2,1},{3,2},{4,3},{5,4},{6,5},{7,6},{9,8},{10,9},{11,10},{12... | collective-permute-start | bytes 1572872 | tf_op jit(solution)/shard_map/ppermute | solution.py:37
  119.5 37.2 %collective-permute-start.4 = (bf16[256,16,64]{0,2,1:T(8,128)(2,1)}, bf16[256,16,64]{0,2,1:T(8,128)(2,1)S(1)}, u32[]{:S(2)}, u32[]{:S(2)}) collective-permute-start(bf16[256,16,64]{0,2,1:T(8,128)(2,1)} %collective-permute-done), channel_id=1, source_target_pairs={{0,1},{1,2},{2,3},{3,4},{4,5},{5,6},{6,7},{8,9},{9,10},{10,11},{11... | collective-permute-start | bytes 1572872 | tf_op jit(solution)/shard_map/ppermute | solution.py:37
  124.1 43.5 %collective-permute-start.7 = (bf16[256,16,64]{0,2,1:T(8,128)(2,1)}, bf16[256,16,64]{0,2,1:T(8,128)(2,1)S(1)}, u32[]{:S(2)}, u32[]{:S(2)}) collective-permute-start(bf16[256,16,64]{0,2,1:T(8,128)(2,1)} %collective-permute-done.3), channel_id=1, source_target_pairs={{1,0},{2,1},{3,2},{4,3},{5,4},{6,5},{7,6},{9,8},{10,9},{11,10},{12... | collective-permute-start | bytes 1572872 | tf_op jit(solution)/shard_map/ppermute | solution.py:37
  125.4 45.9 %collective-permute-start.5 = (bf16[256,16,64]{0,2,1:T(8,128)(2,1)}, bf16[256,16,64]{0,2,1:T(8,128)(2,1)S(1)}, u32[]{:S(2)}, u32[]{:S(2)}) collective-permute-start(bf16[256,16,64]{0,2,1:T(8,128)(2,1)} %collective-permute-done.1), channel_id=1, source_target_pairs={{0,1},{1,2},{2,3},{3,4},{4,5},{5,6},{6,7},{8,9},{9,10},{10,11},{11... | collective-permute-start | bytes 1572872 | tf_op jit(solution)/shard_map/ppermute | solution.py:37
  132.4 36.7 %copy-start = (f32[16,256,256]{1,2,0:T(8,128)}, f32[16,256,256]{1,2,0:T(8,128)S(1)}, u32[]{:S(2)}) copy-start(f32[16,256,256]{1,2,0:T(8,128)S(1)} %get-tuple-element.46) | copy-start | bytes 12582916
  133.3 32.2 %copy-start.6 = (f32[16,256,256]{1,2,0:T(8,128)}, f32[16,256,256]{1,2,0:T(8,128)S(1)}, u32[]{:S(2)}) copy-start(f32[16,256,256]{1,2,0:T(8,128)S(1)} %get-tuple-element.44) | copy-start | bytes 12582916
  157.6 14.2 %copy-start.10 = (f32[16,256,256]{1,2,0:T(8,128)}, f32[16,256,256]{1,2,0:T(8,128)S(1)}, u32[]{:S(2)}) copy-start(f32[16,256,256]{1,2,0:T(8,128)S(1)} %get-tuple-element.42) | copy-start | bytes 12582916
  158.5 9.1 %copy-start.13 = (f32[16,256,256]{1,2,0:T(8,128)}, f32[16,256,256]{1,2,0:T(8,128)S(1)}, u32[]{:S(2)}) copy-start(f32[16,256,256]{1,2,0:T(8,128)S(1)} %get-tuple-element.40) | copy-start | bytes 12582916
  177.4 13.0 %copy-start.54 = (f32[256]{0:T(256)}, f32[256]{0:T(256)S(1)}, u32[]{:S(2)}) copy-start(f32[256]{0:T(256)S(1)} %broadcast_multiply_fusion.1) | copy-start | bytes 3076
  177.6 12.7 %copy-start.60 = (f32[256]{0:T(256)}, f32[256]{0:T(256)S(1)}, u32[]{:S(2)}) copy-start(f32[256]{0:T(256)S(1)} %fusion.210) | copy-start | bytes 3076
  198.3 25.4 %copy-start.29 = (bf16[1,256,1024]{2,1,0:T(8,128)(2,1)S(1)}, bf16[1,256,1024]{2,1,0:T(8,128)(2,1)}, u32[]{:S(2)}) copy-start(bf16[1,256,1024]{2,1,0:T(8,128)(2,1)} %param.21) | copy-start | bytes 1572868
  209.4 14.3 %copy-start.51 = (f32[1024]{0:T(1024)S(1)}, f32[1024]{0:T(1024)}, u32[]{:S(2)}) copy-start(f32[1024]{0:T(1024)} %convert_element_type.255) | copy-start | bytes 12292
  209.4 15.2 %copy-start.52 = (f32[1024]{0:T(1024)S(1)}, f32[1024]{0:T(1024)}, u32[]{:S(2)}) copy-start(f32[1024]{0:T(1024)} %convert_element_type.256) | copy-start | bytes 12292
  281.9 16.7 %copy-start.19 = (bf16[256,1024]{0,1:T(8,128)(2,1)S(1)}, bf16[256,1024]{0,1:T(8,128)(2,1)}, u32[]{:S(2)}) copy-start(bf16[256,1024]{0,1:T(8,128)(2,1)} %copy-done.18) | copy-start | bytes 1572868
  283.3 15.7 %copy-start.17 = (bf16[16,256,64]{1,2,0:T(8,128)(2,1)S(1)}, bf16[16,256,64]{1,2,0:T(8,128)(2,1)}, u32[]{:S(2)}) copy-start(bf16[16,256,64]{1,2,0:T(8,128)(2,1)} %fusion.152) | copy-start | bytes 1572868
  284.9 28.8 %collective-permute-start.10 = (bf16[256,16,64]{0,2,1:T(8,128)(2,1)}, bf16[256,16,64]{0,2,1:T(8,128)(2,1)}, u32[]{:S(2)}, u32[]{:S(2)}) collective-permute-start(bf16[256,16,64]{0,2,1:T(8,128)(2,1)} %fusion.167), channel_id=1, source_target_pairs={{1,0},{2,1},{3,2},{4,3},{5,4},{6,5},{7,6},{9,8},{10,9},{11,10},{12... | collective-permute-start | bytes 1572872 | tf_op jit(solution)/shard_map/ppermute | solution.py:37
  286.2 44.6 %collective-permute-start.14 = (bf16[256,16,64]{0,2,1:T(8,128)(2,1)}, bf16[256,16,64]{0,2,1:T(8,128)(2,1)}, u32[]{:S(2)}, u32[]{:S(2)}) collective-permute-start(bf16[256,16,64]{0,2,1:T(8,128)(2,1)} %fusion.171), channel_id=1, source_target_pairs={{1,0},{2,1},{3,2},{4,3},{5,4},{6,5},{7,6},{9,8},{10,9},{11,10},{12... | collective-permute-start | bytes 1572872 | tf_op jit(solution)/shard_map/ppermute | solution.py:37
  287.5 37.1 %collective-permute-start.12 = (bf16[256,16,64]{0,2,1:T(8,128)(2,1)}, bf16[256,16,64]{0,2,1:T(8,128)(2,1)}, u32[]{:S(2)}, u32[]{:S(2)}) collective-permute-start(bf16[256,16,64]{0,2,1:T(8,128)(2,1)} %fusion.166), channel_id=1, source_target_pairs={{0,1},{1,2},{2,3},{3,4},{4,5},{5,6},{6,7},{8,9},{9,10},{10,11},{11... | collective-permute-start | bytes 1572872 | tf_op jit(solution)/shard_map/ppermute | solution.py:37
  293.5 54.0 %collective-permute-start.16 = (bf16[256,16,64]{0,2,1:T(8,128)(2,1)}, bf16[256,16,64]{0,2,1:T(8,128)(2,1)}, u32[]{:S(2)}, u32[]{:S(2)}) collective-permute-start(bf16[256,16,64]{0,2,1:T(8,128)(2,1)} %fusion.168), channel_id=1, source_target_pairs={{0,1},{1,2},{2,3},{3,4},{4,5},{5,6},{6,7},{8,9},{9,10},{10,11},{11... | collective-permute-start | bytes 1572872 | tf_op jit(solution)/shard_map/ppermute | solution.py:37
  313.6 17.1 %copy-start.1 = (f32[16,256,256]{1,2,0:T(8,128)S(1)}, f32[16,256,256]{1,2,0:T(8,128)}, u32[]{:S(2)}) copy-start(f32[16,256,256]{1,2,0:T(8,128)} %copy-done) | copy-start | bytes 12582916
  315.6 38.6 %collective-permute-start.11 = (bf16[256,16,64]{0,2,1:T(8,128)(2,1)S(1)}, bf16[256,16,64]{0,2,1:T(8,128)(2,1)S(1)}, u32[]{:S(2)}, u32[]{:S(2)}) collective-permute-start(bf16[256,16,64]{0,2,1:T(8,128)(2,1)S(1)} %add_convert_fusion.11), channel_id=1, source_target_pairs={{1,0},{2,1},{3,2},{4,3},{5,4},{6,5},{7,6},{9,8},{10,9},{11,10},{12... | collective-permute-start | bytes 1572872 | tf_op jit(solution)/shard_map/ppermute | solution.py:37
  326.3 43.6 %collective-permute-start.13 = (bf16[256,16,64]{0,2,1:T(8,128)(2,1)S(1)}, bf16[256,16,64]{0,2,1:T(8,128)(2,1)S(1)}, u32[]{:S(2)}, u32[]{:S(2)}) collective-permute-start(bf16[256,16,64]{0,2,1:T(8,128)(2,1)S(1)} %add_convert_fusion.10), channel_id=1, source_target_pairs={{0,1},{1,2},{2,3},{3,4},{4,5},{5,6},{6,7},{8,9},{9,10},{10,11},{11... | collective-permute-start | bytes 1572872 | tf_op jit(solution)/shard_map/ppermute | solution.py:37
  332.9 37.3 %copy-start.28 = (bf16[1024,1024]{1,0:T(8,128)(2,1)S(1)}, bf16[1024,1024]{1,0:T(8,128)(2,1)}, u32[]{:S(2)}) copy-start(bf16[1024,1024]{1,0:T(8,128)(2,1)} %all-gather.8.cloned.1.call-done) | copy-start | bytes 6291460
  332.9 38.1 %collective-permute-start.15 = (bf16[256,16,64]{0,2,1:T(8,128)(2,1)S(1)}, bf16[256,16,64]{0,2,1:T(8,128)(2,1)S(1)}, u32[]{:S(2)}, u32[]{:S(2)}) collective-permute-start(bf16[256,16,64]{0,2,1:T(8,128)(2,1)S(1)} %add_convert_fusion.8), channel_id=1, source_target_pairs={{1,0},{2,1},{3,2},{4,3},{5,4},{6,5},{7,6},{9,8},{10,9},{11,10},{12... | collective-permute-start | bytes 1572872 | tf_op jit(solution)/shard_map/ppermute | solution.py:37
  349.7 31.4 %copy-start.37 = (f32[256,16,64]{0,2,1:T(8,128)S(1)}, f32[256,16,64]{0,2,1:T(8,128)}, u32[]{:S(2)}) copy-start(f32[256,16,64]{0,2,1:T(8,128)} %fusion.104) | copy-start | bytes 3145732
  349.7 31.4 %collective-permute-start.17 = (bf16[256,16,64]{0,2,1:T(8,128)(2,1)S(1)}, bf16[256,16,64]{0,2,1:T(8,128)(2,1)S(1)}, u32[]{:S(2)}, u32[]{:S(2)}) collective-permute-start(bf16[256,16,64]{0,2,1:T(8,128)(2,1)S(1)} %add_convert_fusion.7), channel_id=1, source_target_pairs={{0,1},{1,2},{2,3},{3,4},{4,5},{5,6},{6,7},{8,9},{9,10},{10,11},{11... | collective-permute-start | bytes 1572872 | tf_op jit(solution)/shard_map/ppermute | solution.py:37
  370.2 11.1 %copy-start.27 = (bf16[1024,1024]{1,0:T(8,128)(2,1)S(1)}, bf16[1024,1024]{1,0:T(8,128)(2,1)}, u32[]{:S(2)}) copy-start(bf16[1024,1024]{1,0:T(8,128)(2,1)} %all-gather.10.cloned.1.call-done) | copy-start | bytes 6291460
  (53 other events, 202.7 us)
Sparse Core Ops, SparseCore 0:
  9.7 34.0 all-gather.7
  45.4 33.2 all-gather.9
  80.3 33.9 all-gather.5
  115.7 33.9 all-gather.11
  151.1 58.2 all-gather.13
  300.5 141.7 all-reduce.2
